TPU v7x, 256 devices: a whole 4x4x8 slice. The times are simulated.
256 devices in a mesh: dp: 8 (over y, z_hi), mp: 32 (over z_lo, x, core).
Axes of the slice: x: 4, y: 4, z: 8 (z_hi: 2, z_lo: 4; z = z_hi * 4 + z_lo), core: 2. Of those that a mesh axis runs over, the one named last changes fastest.
Arguments:
- features: bfloat16 [256, 1280, 1024], P('dp', 'mp'), may hold values from -6 to 6
- conv_weight: bfloat16 [1280, 1280], P('mp'), may hold values from -0.15625 to 0.15625
- norm_gain: float32 [1280], replicated, may hold values from 0.25 to 1.75
- norm_bias: float32 [1280], replicated, may hold values from -3 to 3
- logit_vector: float32 [1280], replicated, may hold values from -0.625 to 0.625
- labels: int32 [256], P(('dp', 'mp')), may hold values 0 or 1
Outputs:
- grad_features: float32 [256, 1280, 1024], P('dp', 'mp')
- grad_weight: float32 [1280, 1280], P('mp')
- head_grads: float32 [3, 1280], replicated
- loss: float32 [], replicated
All inputs are finite; a program needn't handle non-finite values. No bound on the sum of `labels` on one device may be relied on, other than what follows from the above.
Results may differ from a plain program's by a relative error of at most 0.0029.
Values may be sent and summed in bfloat16 or wider, within the bound.
A program may use at most 128 MiB of HBM per device.

v0:
```python
import jax
import jax.numpy as jnp
from jax import lax
from jax.sharding import Mesh
from jax.sharding import PartitionSpec as P

GROUPS = 32
MP = ("mp_0", "mp_1", "mp_2")
DP = ("dp_0", "dp_1")
DP_MP = ("dp_0", "dp_1", "mp_0", "mp_1", "mp_2")
norm_eps = 1e-05


def from_everyone(x, axis):
    copies = jnp.broadcast_to(x, (lax.axis_size(axis), *x.shape))
    return lax.all_to_all(copies, axis, split_axis=0, concat_axis=0, tiled=True)


def taken_together(x, axis):
    return from_everyone(x, axis).sum(axis=0)


def head_total(pre, norm_gain, norm_bias, logit_vector, signs):
    images, channels, cell_count = pre.shape
    grouped = pre.reshape(images, GROUPS, channels // GROUPS, cell_count)
    center = jnp.mean(grouped, axis=(2, 3), keepdims=True)
    spread = jnp.mean((grouped - center) ** 2, axis=(2, 3), keepdims=True)
    normed = ((grouped - center) * lax.rsqrt(spread + norm_eps)).reshape(
        images, channels, cell_count
    )
    normed = normed * norm_gain[:, None] + norm_bias[:, None]
    hidden = jax.nn.silu(normed)
    logits = (
        jnp.einsum("c,ncs->n", logit_vector, hidden, precision=lax.Precision.HIGHEST) / cell_count
    )
    margin = jnp.maximum(1.0 - signs * logits, 0.0)
    return jnp.sum(margin * margin)


def shards(features, conv_weight, norm_gain, norm_bias, logit_vector, labels):
    signs = 2.0 * labels.astype(jnp.float32) - 1.0
    weight_full = lax.all_gather(conv_weight, MP, axis=0, tiled=True)
    image_block = lax.all_to_all(features, MP, split_axis=0, concat_axis=1, tiled=True)
    pre = jnp.einsum("io,nis->nos", weight_full, image_block, preferred_element_type=jnp.float32)
    total, pull = jax.vjp(
        lambda p, g, b, h: head_total(p, g, b, h, signs), pre, norm_gain, norm_bias, logit_vector
    )
    grad_pre, grad_gain, grad_bias, grad_vec = pull(jnp.ones((), jnp.float32))
    grad_pre = grad_pre.astype(jnp.bfloat16)
    grad_image = jnp.einsum(
        "io,nos->nis", weight_full, grad_pre, preferred_element_type=jnp.float32
    )
    grad_features = lax.all_to_all(
        grad_image.astype(jnp.bfloat16), MP, split_axis=1, concat_axis=0, tiled=True
    ).astype(jnp.float32)
    weight_term = jnp.einsum(
        "nis,nos->io", image_block, grad_pre, preferred_element_type=jnp.float32
    )
    weight_rows = lax.psum_scatter(weight_term, MP, scatter_dimension=0, tiled=True)
    grad_weight = taken_together(weight_rows, DP)
    small = jnp.stack([grad_gain, grad_bias, grad_vec, jnp.full_like(grad_gain, total)])
    small = lax.psum(small, DP_MP)
    total_sum, head_grads = (small[3, 0], small[:3])
    image_total = pre.shape[0] * lax.axis_size(DP) * lax.axis_size(MP)
    loss = total_sum / image_total
    return (grad_features, grad_weight, head_grads, loss)


def solution(mesh):
    finer = Mesh(mesh.devices.reshape(4, 2, 4, 4, 2), ("dp_0", "dp_1", "mp_0", "mp_1", "mp_2"))
    placed = (P(DP, MP, None), P(MP, None), P(), P(), P(), P(DP_MP))
    return jax.shard_map(
        shards,
        mesh=finer,
        in_specs=placed,
        out_specs=(P(DP, MP, None), P(MP, None), P(), P()),
        check_vma=False,
    )
```

profile of v0, /device:TPU:1, one launch (start us, length us, event | category | flops | bytes accessed | tf_op | source)
XLA Modules:
  0.0 425.3 jit_solution(12105964118553905364)
XLA Ops:
  7.2 0.7 all-gather.2.cloned.1.call-update
  7.9 10.0 %all-to-all-start = ((bf16[32,40,1024]{2,1,0:T(8,128)(2,1)}), bf16[32,40,1024]{2,1,0:T(8,128)(2,1)S(1)}, u32[]{:S(2)}, u32[]{:S(2)}) async-start(bf16[32,40,1024]{2,1,0:T(8,128)(2,1)} %param.6), calls=%async_computation | async-start | bytes 5242880 | tf_op jit(solution)/shard_map/all_to_all | solution.py:43
  18.6 74.4 %all-to-all-done = bf16[32,40,1024]{2,1,0:T(8,128)(2,1)S(1)} async-done(((bf16[32,40,1024]{2,1,0:T(8,128)(2,1)}), bf16[32,40,1024]{2,1,0:T(8,128)(2,1)S(1)}, u32[]{:S(2)}, u32[]{:S(2)}) %all-to-all-start) | async-done | bytes 2621472 | tf_op jit(solution)/shard_map/all_to_all | solution.py:43
  93.0 4.4 %all-gather.2.cloned.1.call-done = bf16[1280,1280]{1,0:T(8,128)(2,1)} async-done(((bf16[40,1280]{1,0:T(8,128)(2,1)}), bf16[1280,1280]{1,0:T(8,128)(2,1)}) %all-gather.2.cloned.1.call-update) | async-done | bytes 3276816 | tf_op jit(solution)/shard_map/all_gather | solution.py:42
  97.4 7.3 %fusion.11 = (f32[1280]{0:T(1024)S(1)}, f32[1024,1280]{1,0:T(8,128)}) fusion(bf16[1280,1024]{1,0:T(8,128)(2,1)S(1)} %bitcast.93, bf16[1280,1280]{1,0:T(8,128)(2,1)} %all-gather.2.cloned.1.call-done), kind=kOutput, calls=%fused_computation.31 | convolution fusion | flops 3356752640 | bytes 11146240 | tf_op jit(solution)/shard_map/io,nis->nos/dot_general | solution.py:44
  104.8 0.1 reduce_sum.148
  105.1 3.1 fusion.2
  108.3 0.1 reduce_sum.151
  108.6 4.2 multiply_reduce_fusion.1
  112.8 0.6 multiply_reduce_fusion.3
  114.1 5.7 %multiply_reduce_fusion = (f32[1280]{0:T(1024)S(1)}, f32[1280]{0:T(1024)S(1)}, f32[1280]{0:T(1024)S(1)}, f32[1280]{0:T(1024)S(1)}) fusion(f32[1024,1280]{1,0:T(8,128)} %get-tuple-element.13, f32[1280]{0:T(1024)S(1)} %mul.156, f32[1280]{0:T(1024)S(1)} %sub.53, f32[1280]{0:T(1024)S(1)} %copy-done, f32[1280]{0:T(1024)S(1)} %copy-done.1, ...), kind=kLoop, calls=%fused_computation.11 | loop fusion | flops 27520000 | bytes 5288960 | tf_op jit(solution)/shard_map/transpose(jvp())/reduce_sum | solution.py:31
  119.9 0.1 reduce_sum.158
  120.1 0.1 reduce_sum.155
  120.4 3.1 fusion.4
  123.6 0.1 reduce_sum.161
  123.9 11.6 %convolution_bitcast_fusion = f32[1280,1280]{0,1:T(8,128)} fusion(bf16[1280,1024]{1,0:T(8,128)(2,1)S(1)} %bitcast.94, f32[1024,1280]{1,0:T(8,128)} %get-tuple-element.13, f32[1280]{0:T(1024)S(1)} %broadcast_in_dim.24, f32[1280]{0:T(1024)S(1)} %mul.178, f32[1280]{0:T(1024)S(1)} %copy-done.1, f32[1280]{0:T(1024)S(1)} %mul.156, f32[1280]{0:T(1024)S(1)} %sub.53, ...), kind=kOutput, calls=%fused_computation | convolution fusion | flops 3380346880 | bytes 14453760 | tf_op jit(solution)/shard_map/nis,nos->io/dot_general | solution.py:56
  135.5 8.2 %copy.22 = f32[1280,1280]{1,0:T(8,128)} copy(f32[1280,1280]{0,1:T(8,128)} %convolution_bitcast_fusion) | data formatting | bytes 13107200
  143.7 9.8 %fusion.5 = bf16[1,1280,1024]{1,2,0:T(8,128)(2,1)S(1)} fusion(bf16[1280,1280]{1,0:T(8,128)(2,1)} %all-gather.2.cloned.1.call-done, f32[1024,1280]{1,0:T(8,128)} %get-tuple-element.13, f32[1280]{0:T(1024)S(1)} %broadcast_in_dim.24, f32[1280]{0:T(1024)S(1)} %mul.178, f32[1280]{0:T(1024)S(1)} %copy-done.1, f32[1280]{0:T(1024)S(1)} %mul.156, ...), kind=kOutput, calls=%fused_computation.19 | convolution fusion | flops 3381657600 | bytes 11176960 | tf_op jit(solution)/shard_map/io,nos->nis/dot_general | solution.py:50
  153.5 7.9 %copy.17 = bf16[1,1280,1024]{2,0,1:T(2,128)(2,1)} copy(bf16[1,1280,1024]{1,2,0:T(8,128)(2,1)S(1)} %fusion.5) | data formatting | bytes 5242880 | tf_op jit(solution)/shard_map/convert_element_type | solution.py:54
  161.4 0.5 broadcast.211
  161.9 15.6 %reduce.26 = bf16[1280,1024]{1,0:T(8,128)(2,1)S(1)} reduce(bf16[1280,1,1024]{2,1,0:T(2,128)(2,1)} %bitcast.90, bf16[]{:T(256)} %broadcast.211), dimensions={1}, to_apply=%bitcast.83.reduce_sub_computation | reduce | bytes 5242882
  177.5 2.9 reshape.373
  180.4 78.7 %all_to_all.23 = bf16[32,2,20480]{2,1,0:T(2,128)(2,1)S(1)} all-to-all(bf16[32,2,20480]{2,1,0:T(2,128)(2,1)} %reshape.373), channel_id=1, replica_groups=mesh['dp_0'=4,'dp_1'=2,'mp_0'=4,'mp_1'=4,'mp_2'=2] {'mp_0','mp_1','mp_2'}, dimensions={0} | all-to-all | bytes 5242880 | tf_op jit(solution)/shard_map/all_to_all | solution.py:53
  259.1 43.7 %reduce-scatter.4.cloned.1.call-done = f32[40,1280]{1,0:T(8,128)} async-done(((f32[1280,1280]{1,0:T(8,128)}), f32[40,1280]{1,0:T(8,128)}) %reduce-scatter.4.cloned.1.call-update) | async-done | bytes 204816 | tf_op jit(solution)/shard_map/reduce_scatter | solution.py:59
  302.7 2.2 broadcast_in_dim.26
  305.0 7.4 %all-to-all-start.2 = ((f32[8,40,1280]{2,1,0:T(8,128)}), f32[8,40,1280]{2,1,0:T(8,128)}, u32[]{:S(2)}, u32[]{:S(2)}) async-start(f32[8,40,1280]{2,1,0:T(8,128)} %broadcast_in_dim.26), calls=%async_computation.2 | async-start | bytes 3276800 | tf_op jit(solution)/shard_map/all_to_all | solution.py:16
  312.6 87.7 %psum.7 = f32[4,1280]{1,0:T(4,128)S(1)} all-reduce(f32[4,1280]{1,0:T(4,128)S(1)} %maximum_maximum_fusion), channel_id=1, replica_groups=mesh['dp_0'=4,'dp_1'=2,'mp_0'=4,'mp_1'=4,'mp_2'=2] {'dp_0','dp_1','mp_0'..., use_global_device_ids=true, to_apply=%region_15.16 | all-reduce | flops 5120 | bytes 40960 | tf_op jit(solution)/shard_map/psum | solution.py:62
  400.3 0.5 slice.9
  401.5 7.2 %reshape.374 = bf16[1280,1,1024]{2,1,0:T(2,128)(2,1)} reshape(bf16[32,2,20480]{2,1,0:T(2,128)(2,1)S(1)} %all_to_all.23) | data formatting | bytes 5242880
  408.6 3.5 copy.18
  412.2 3.0 convert.1
  415.2 2.2 reduce_sum.162
  (36 shorter events, 1.4 us)
Async XLA Ops:
  7.2 90.3 %all-gather.2.cloned.1.call-start = ((), (), s32[]{:S(2)}) async-start(), calls=%async_computation.4 | async-start | bytes 3379200 | tf_op jit(solution)/shard_map/all_gather | solution.py:42
  7.9 85.1 %all-to-all-start = ((bf16[32,40,1024]{2,1,0:T(8,128)(2,1)}), bf16[32,40,1024]{2,1,0:T(8,128)(2,1)S(1)}, u32[]{:S(2)}, u32[]{:S(2)}) async-start(bf16[32,40,1024]{2,1,0:T(8,128)(2,1)} %param.6), calls=%async_computation | async-start | bytes 5242880 | tf_op jit(solution)/shard_map/all_to_all | solution.py:43
  17.9 284.8 %reduce-scatter.4.cloned.1.call-start = ((), (), s32[]{:S(2)}) async-start(), calls=%async_computation.5 | async-start | bytes 6758400 | tf_op jit(solution)/shard_map/reduce_scatter | solution.py:59
  104.8 3.9 copy-start
  104.8 3.9 copy-start.1
  105.1 7.7 %copy-start.2 = (f32[1280]{0:T(1024)S(1)}, f32[1280]{0:T(1024)}, u32[]{:S(2)}) copy-start(f32[1280]{0:T(1024)} %param.10) | copy-start | bytes 15364
  305.0 110.2 %all-to-all-start.2 = ((f32[8,40,1280]{2,1,0:T(8,128)}), f32[8,40,1280]{2,1,0:T(8,128)}, u32[]{:S(2)}, u32[]{:S(2)}) async-start(f32[8,40,1280]{2,1,0:T(8,128)} %broadcast_in_dim.26), calls=%async_computation.2 | async-start | bytes 3276800 | tf_op jit(solution)/shard_map/all_to_all | solution.py:16
  400.3 11.9 %copy-start.3 = (f32[4,1280]{1,0:T(4,128)}, f32[4,1280]{1,0:T(4,128)S(1)}, u32[]{:S(2)}) copy-start(f32[4,1280]{1,0:T(4,128)S(1)} %psum.7) | copy-start | bytes 61444
Sparse Core Ops, SparseCore 0:
  9.8 87.5 all-gather.1
  143.9 158.8 reduce-scatter.3
where the time goes:
time: 426 us; the launch traced here: 425 us
  blocking collectives  166 us (39%)
  waiting for transfers between devices  123 us (29%)
  other arithmetic  38.1 us (9%)
  local copies, waits for them, and re-layouts  34.1 us (8%)
  matrix products  28.7 us (7%)
  starting transfers between devices  17.5 us (4%)
  between operations  17.3 us (4%)
    psum x1, blocking collectives, shards(): small = lax.psum(small, DP_MP)  87.7 us
    all_to_all x1, blocking collectives, shards(): lax.all_to_all(grad_image.astype(jnp.bfloat16), MP, split_axis=1, concat_...  78.7 us
    all_to_all x1, waiting for transfers between devices, shards(): lax.all_to_all(features, MP, split_axis=0, concat_axis=1, tiled=True)  74.4 us
    reduce_scatter x1, waiting for transfers between devices, shards(): lax.psum_scatter(weight_term, MP, scatter_dimension=0, tiled=True)  43.7 us
    unnamed x12, local copies, waits for them, and re-layouts  18.8 us
    unnamed x1, other arithmetic  15.6 us
    dot_general x1, matrix products, shards(): jnp.einsum('nis,nos->io', image_block, grad_pre, preferred_element_type=j...  11.6 us
    all_to_all x1, starting transfers between devices, shards(): lax.all_to_all(features, MP, split_axis=0, concat_axis=1, tiled=True)  10 us
  transfers between devices with their start and end apart: 4, of which 3 were waited for; matrix products, arithmetic and copies ran while one was open for 12% of the time, Pallas kernels for 0%

commit v1 on v0

--- a/solution.py
+++ b/solution.py
@@ -50,9 +50,19 @@
     grad_image = jnp.einsum(
         "io,nos->nis", weight_full, grad_pre, preferred_element_type=jnp.float32
     )
-    grad_features = lax.all_to_all(
-        grad_image.astype(jnp.bfloat16), MP, split_axis=1, concat_axis=0, tiled=True
-    ).astype(jnp.float32)
+
+    def serve_results(local_x):
+        return jnp.concatenate(
+            lax.all_to_all(
+                jnp.stack(jnp.split(local_x, lax.axis_size(MP), axis=1)),
+                axis_name=MP,
+                split_axis=0,
+                concat_axis=0,
+            ),
+            axis=0,
+        )
+
+    grad_features = serve_results(grad_image.astype(jnp.bfloat16)).astype(jnp.float32)
     weight_term = jnp.einsum(
         "nis,nos->io", image_block, grad_pre, preferred_element_type=jnp.float32
     )

time: 426 us -> 416 us (0.977)
  local copies, waits for them, and re-layouts: 34.1 us -> 58.2 us
  waiting for transfers between devices: 123 us -> 104 us
  other arithmetic: 38.1 us -> 22.6 us
    another operation x0 -> x35, local copies, waits for them, and re-layouts: none -> 37.9 us  [serve_results(): jnp.stack(jnp.split(local_x, lax.axis_size(MP), axis=1))]
    reduce_scatter x1, waiting for transfers between devices: 43.7 us -> 23.8 us  [shards(): lax.psum_scatter(weight_term, MP, scatter_dimension=0, tiled=True)]
    unnamed x1 -> x0, other arithmetic: 15.6 us -> none
    convert_element_type x1 -> x0, local copies, waits for them, and re-layouts: 7.87 us -> none  [shards(): grad_image.astype(jnp.bfloat16)]
    unnamed x12 -> x68, local copies, waits for them, and re-layouts: 18.8 us -> 16.5 us
  transfers between devices with their start and end apart: 4 -> 4, of which waited for: 3 -> 3; matrix products, arithmetic and copies ran while one was open for 12% -> 14% of each run, Pallas kernels for 0% -> 0%
where the time goes in v1:
time: 416 us; the launch traced here: 415 us
  blocking collectives  166 us (40%)
  waiting for transfers between devices  104 us (25%)
  local copies, waits for them, and re-layouts  58.2 us (14%)
  matrix products  28.7 us (7%)
  other arithmetic  22.6 us (5%)
  starting transfers between devices  17.9 us (4%)
  between operations  17.8 us (4%)
    psum x1, blocking collectives, shards(): small = lax.psum(small, DP_MP)  87.3 us
    all_to_all x1, blocking collectives, serve_results(): lax.all_to_all(jnp.stack(jnp.split(local_x, lax.axis_size(MP), axis=1)),...  78.6 us
    all_to_all x1, waiting for transfers between devices, shards(): lax.all_to_all(features, MP, split_axis=0, concat_axis=1, tiled=True)  74.3 us
    another operation x35, local copies, waits for them, and re-layouts, serve_results(): jnp.stack(jnp.split(local_x, lax.axis_size(MP), axis=1))  37.9 us
    reduce_scatter x1, waiting for transfers between devices, shards(): lax.psum_scatter(weight_term, MP, scatter_dimension=0, tiled=True)  23.8 us
    unnamed x68, local copies, waits for them, and re-layouts  16.5 us
    dot_general x1, matrix products, shards(): jnp.einsum('nis,nos->io', image_block, grad_pre, preferred_element_type=j...  11.6 us
    all_to_all x1, starting transfers between devices, shards(): lax.all_to_all(features, MP, split_axis=0, concat_axis=1, tiled=True)  10 us
  transfers between devices with their start and end apart: 4, of which 3 were waited for; matrix products, arithmetic and copies ran while one was open for 14% of the time, Pallas kernels for 0%

profile of v1, /device:TPU:1, one launch (start us, length us, event | category | flops | bytes accessed | tf_op | source)
XLA Modules:
  0.0 414.9 jit_solution(16568277558384576949)
XLA Ops:
  7.9 10.0 %all-to-all-start = ((bf16[32,40,1024]{2,1,0:T(8,128)(2,1)}), bf16[32,40,1024]{2,1,0:T(8,128)(2,1)S(1)}, u32[]{:S(2)}, u32[]{:S(2)}) async-start(bf16[32,40,1024]{2,1,0:T(8,128)(2,1)} %param.6), calls=%async_computation | async-start | bytes 5242880 | tf_op jit(solution)/shard_map/all_to_all | solution.py:43
  18.6 74.3 %all-to-all-done = bf16[32,40,1024]{2,1,0:T(8,128)(2,1)S(1)} async-done(((bf16[32,40,1024]{2,1,0:T(8,128)(2,1)}), bf16[32,40,1024]{2,1,0:T(8,128)(2,1)S(1)}, u32[]{:S(2)}, u32[]{:S(2)}) %all-to-all-start) | async-done | bytes 2621472 | tf_op jit(solution)/shard_map/all_to_all | solution.py:43
  92.9 5.0 %all-gather.2.cloned.1.call-done = bf16[1280,1280]{1,0:T(8,128)(2,1)} async-done(((bf16[40,1280]{1,0:T(8,128)(2,1)}), bf16[1280,1280]{1,0:T(8,128)(2,1)}) %all-gather.2.cloned.1.call-update) | async-done | bytes 3276816 | tf_op jit(solution)/shard_map/all_gather | solution.py:42
  97.9 7.3 %fusion.11 = (f32[1280]{0:T(1024)S(1)}, f32[1024,1280]{1,0:T(8,128)}) fusion(bf16[1280,1024]{1,0:T(8,128)(2,1)S(1)} %bitcast.153, bf16[1280,1280]{1,0:T(8,128)(2,1)} %all-gather.2.cloned.1.call-done), kind=kOutput, calls=%fused_computation.96 | convolution fusion | flops 3356752640 | bytes 11146240 | tf_op jit(solution)/shard_map/io,nis->nos/dot_general | solution.py:44
  105.6 3.1 fusion.2
  109.1 4.2 %multiply_reduce_fusion.1 = f32[1280]{0:T(1024)S(1)} fusion(f32[1024,1280]{1,0:T(8,128)} %get-tuple-element.45, f32[1280]{0:T(1024)S(1)} %copy-done.14, f32[1280]{0:T(1024)S(1)} %copy-done.15, f32[1280]{0:T(1024)S(1)} %mul.156, f32[1280]{0:T(1024)S(1)} %sub.53), kind=kLoop, calls=%fused_computation.13 | loop fusion | flops 11795200 | bytes 5268480 | tf_op jit(solution)/shard_map/jvp(c,ncs->n)/reduce_sum | solution.py:34
  114.6 5.7 %multiply_reduce_fusion = (f32[1280]{0:T(1024)S(1)}, f32[1280]{0:T(1024)S(1)}, f32[1280]{0:T(1024)S(1)}, f32[1280]{0:T(1024)S(1)}) fusion(f32[1024,1280]{1,0:T(8,128)} %get-tuple-element.45, f32[1280]{0:T(1024)S(1)} %mul.156, f32[1280]{0:T(1024)S(1)} %sub.53, f32[1280]{0:T(1024)S(1)} %copy-done.14, f32[1280]{0:T(1024)S(1)} %copy-done.15, ...), kind=kLoop, calls=%fused_computation.11 | loop fusion | flops 27520000 | bytes 5288960 | tf_op jit(solution)/shard_map/transpose(jvp())/reduce_sum | solution.py:31
  120.9 3.1 fusion.4
  124.3 11.6 %convolution_bitcast_fusion = f32[1280,1280]{0,1:T(8,128)} fusion(bf16[1280,1024]{1,0:T(8,128)(2,1)S(1)} %bitcast.154, f32[1024,1280]{1,0:T(8,128)} %get-tuple-element.45, f32[1280]{0:T(1024)S(1)} %broadcast_in_dim.24, f32[1280]{0:T(1024)S(1)} %mul.178, f32[1280]{0:T(1024)S(1)} %copy-done.15, f32[1280]{0:T(1024)S(1)} %mul.156, f32[1280]{0:T(1024)S(1)} %sub.53, ...), kind=kOutput, calls=%fused_computation | convolution fusion | flops 3380346880 | bytes 14453760 | tf_op jit(solution)/shard_map/nis,nos->io/dot_general | solution.py:66
  136.0 8.2 %copy.80 = f32[1280,1280]{1,0:T(8,128)} copy(f32[1280,1280]{0,1:T(8,128)} %convolution_bitcast_fusion) | data formatting | bytes 13107200
  144.2 9.8 %fusion.5 = bf16[1,1280,1024]{1,2,0:T(8,128)(2,1)S(1)} fusion(bf16[1280,1280]{1,0:T(8,128)(2,1)} %all-gather.2.cloned.1.call-done, f32[1024,1280]{1,0:T(8,128)} %get-tuple-element.45, f32[1280]{0:T(1024)S(1)} %broadcast_in_dim.24, f32[1280]{0:T(1024)S(1)} %mul.178, f32[1280]{0:T(1024)S(1)} %copy-done.15, f32[1280]{0:T(1024)S(1)} %mul.156, ...), kind=kOutput, calls=%fused_computation.19 | convolution fusion | flops 3381657600 | bytes 11176960 | tf_op jit(solution)/shard_map/io,nos->nis/dot_general | solution.py:50
  154.0 2.4 slice_bitcast_fusion.19
  157.5 1.7 copy.56
  159.1 1.7 copy.55
  160.8 1.7 copy.54
  162.5 1.7 copy.53
  164.2 1.7 copy.52
  165.9 1.7 copy.51
  167.6 1.7 copy.50
  169.3 1.7 copy.49
  171.0 1.7 copy.48
  175.0 3.4 slice_bitcast_fusion
  185.0 1.7 copy.70
  186.7 1.7 copy.69
  188.4 1.7 copy.68
  200.6 78.6 %all_to_all.19 = bf16[32,1,40,1024]{3,2,1,0:T(8,128)(2,1)S(1)} all-to-all(bf16[32,1,40,1024]{3,2,1,0:T(8,128)(2,1)S(1)} %constant_dynamic-update-slice_fusion), channel_id=1, replica_groups=mesh['dp_0'=4,'dp_1'=2,'mp_0'=4,'mp_1'=4,'mp_2'=2] {'mp_0','mp_1','mp_2'}, dimensions={0} | all-to-all | bytes 5242880 | tf_op jit(solution)/shard_map/all_to_all | solution.py:56
  279.2 23.8 %reduce-scatter.4.cloned.1.call-done = f32[40,1280]{1,0:T(8,128)} async-done(((f32[1280,1280]{1,0:T(8,128)}), f32[40,1280]{1,0:T(8,128)}) %reduce-scatter.4.cloned.1.call-update) | async-done | bytes 204816 | tf_op jit(solution)/shard_map/reduce_scatter | solution.py:69
  303.0 2.2 broadcast_in_dim.26
  305.2 7.8 %all-to-all-start.2 = ((f32[8,40,1280]{2,1,0:T(8,128)}), f32[8,40,1280]{2,1,0:T(8,128)}, u32[]{:S(2)}, u32[]{:S(2)}) async-start(f32[8,40,1280]{2,1,0:T(8,128)} %broadcast_in_dim.26), calls=%async_computation.2 | async-start | bytes 3276800 | tf_op jit(solution)/shard_map/all_to_all | solution.py:16
  313.2 87.3 %psum.7 = f32[4,1280]{1,0:T(4,128)S(1)} all-reduce(f32[4,1280]{1,0:T(4,128)S(1)} %maximum_maximum_fusion), channel_id=1, replica_groups=mesh['dp_0'=4,'dp_1'=2,'mp_0'=4,'mp_1'=4,'mp_2'=2] {'dp_0','dp_1','mp_0'..., use_global_device_ids=true, to_apply=%region_15.16 | all-reduce | flops 5120 | bytes 40960 | tf_op jit(solution)/shard_map/psum | solution.py:72
  401.7 3.0 bitcast_convert_fusion
  404.7 2.2 reduce_sum.162
  (124 shorter events, 23.8 us)
Async XLA Ops:
  7.2 90.7 %all-gather.2.cloned.1.call-start = ((), (), s32[]{:S(2)}) async-start(), calls=%async_computation.4 | async-start | bytes 3379200 | tf_op jit(solution)/shard_map/all_gather | solution.py:42
  7.9 85.0 %all-to-all-start = ((bf16[32,40,1024]{2,1,0:T(8,128)(2,1)}), bf16[32,40,1024]{2,1,0:T(8,128)(2,1)S(1)}, u32[]{:S(2)}, u32[]{:S(2)}) async-start(bf16[32,40,1024]{2,1,0:T(8,128)(2,1)} %param.6), calls=%async_computation | async-start | bytes 5242880 | tf_op jit(solution)/shard_map/all_to_all | solution.py:43
  17.9 285.0 %reduce-scatter.4.cloned.1.call-start = ((), (), s32[]{:S(2)}) async-start(), calls=%async_computation.5 | async-start | bytes 6758400 | tf_op jit(solution)/shard_map/reduce_scatter | solution.py:69
  105.2 3.8 copy-start.14
  105.2 3.8 copy-start.15
  108.7 4.6 %copy-start.16 = (f32[1280]{0:T(1024)S(1)}, f32[1280]{0:T(1024)}, u32[]{:S(2)}) copy-start(f32[1280]{0:T(1024)} %param.10) | copy-start | bytes 15364
  178.3 11.8 %copy-start.6 = (bf16[1,1,40,1024]{2,3,1,0:T(8,128)(2,1)S(1)}, bf16[1,1,40,1024]{2,3,1,0:T(8,128)(2,1)}, u32[]{:S(2)}) copy-start(bf16[1,1,40,1024]{2,3,1,0:T(8,128)(2,1)} %get-tuple-element.21) | copy-start | bytes 245764
  178.3 12.6 %copy-start.5 = (bf16[1,1,40,1024]{2,3,1,0:T(8,128)(2,1)S(1)}, bf16[1,1,40,1024]{2,3,1,0:T(8,128)(2,1)}, u32[]{:S(2)}) copy-start(bf16[1,1,40,1024]{2,3,1,0:T(8,128)(2,1)} %get-tuple-element.22) | copy-start | bytes 245764
  178.3 12.7 %copy-start.4 = (bf16[1,1,40,1024]{2,3,1,0:T(8,128)(2,1)S(1)}, bf16[1,1,40,1024]{2,3,1,0:T(8,128)(2,1)}, u32[]{:S(2)}) copy-start(bf16[1,1,40,1024]{2,3,1,0:T(8,128)(2,1)} %get-tuple-element.23) | copy-start | bytes 245764
  178.3 12.9 %copy-start.3 = (bf16[1,1,40,1024]{2,3,1,0:T(8,128)(2,1)S(1)}, bf16[1,1,40,1024]{2,3,1,0:T(8,128)(2,1)}, u32[]{:S(2)}) copy-start(bf16[1,1,40,1024]{2,3,1,0:T(8,128)(2,1)} %get-tuple-element.24) | copy-start | bytes 245764
  178.4 13.0 %copy-start.2 = (bf16[1,1,40,1024]{2,3,1,0:T(8,128)(2,1)S(1)}, bf16[1,1,40,1024]{2,3,1,0:T(8,128)(2,1)}, u32[]{:S(2)}) copy-start(bf16[1,1,40,1024]{2,3,1,0:T(8,128)(2,1)} %get-tuple-element.25) | copy-start | bytes 245764
  178.4 13.1 %copy-start.1 = (bf16[1,1,40,1024]{2,3,1,0:T(8,128)(2,1)S(1)}, bf16[1,1,40,1024]{2,3,1,0:T(8,128)(2,1)}, u32[]{:S(2)}) copy-start(bf16[1,1,40,1024]{2,3,1,0:T(8,128)(2,1)} %get-tuple-element.26) | copy-start | bytes 245764
  178.4 13.2 %copy-start = (bf16[1,1,40,1024]{2,3,1,0:T(8,128)(2,1)S(1)}, bf16[1,1,40,1024]{2,3,1,0:T(8,128)(2,1)}, u32[]{:S(2)}) copy-start(bf16[1,1,40,1024]{2,3,1,0:T(8,128)(2,1)} %get-tuple-element.27) | copy-start | bytes 245764
  182.8 17.4 %copy-start.9 = (bf16[1,1,40,1024]{3,2,1,0:T(8,128)(2,1)S(1)}, bf16[1,1,40,1024]{3,2,1,0:T(8,128)(2,1)}, u32[]{:S(2)}) copy-start(bf16[1,1,40,1024]{3,2,1,0:T(8,128)(2,1)} %copy.54) | copy-start | bytes 245764
  183.9 16.3 %copy-start.8 = (bf16[1,1,40,1024]{3,2,1,0:T(8,128)(2,1)S(1)}, bf16[1,1,40,1024]{3,2,1,0:T(8,128)(2,1)}, u32[]{:S(2)}) copy-start(bf16[1,1,40,1024]{3,2,1,0:T(8,128)(2,1)} %copy.55) | copy-start | bytes 245764
  183.9 16.3 %copy-start.7 = (bf16[1,1,40,1024]{3,2,1,0:T(8,128)(2,1)S(1)}, bf16[1,1,40,1024]{3,2,1,0:T(8,128)(2,1)}, u32[]{:S(2)}) copy-start(bf16[1,1,40,1024]{3,2,1,0:T(8,128)(2,1)} %copy.56) | copy-start | bytes 245764
  190.9 9.5 %copy-start.13 = (bf16[1,1,40,1024]{3,2,1,0:T(8,128)(2,1)S(1)}, bf16[1,1,40,1024]{3,2,1,0:T(8,128)(2,1)}, u32[]{:S(2)}) copy-start(bf16[1,1,40,1024]{3,2,1,0:T(8,128)(2,1)} %copy.67) | copy-start | bytes 245764
  191.0 9.4 %copy-start.12 = (bf16[1,1,40,1024]{3,2,1,0:T(8,128)(2,1)S(1)}, bf16[1,1,40,1024]{3,2,1,0:T(8,128)(2,1)}, u32[]{:S(2)}) copy-start(bf16[1,1,40,1024]{3,2,1,0:T(8,128)(2,1)} %copy.68) | copy-start | bytes 245764
  191.0 9.4 %copy-start.11 = (bf16[1,1,40,1024]{3,2,1,0:T(8,128)(2,1)S(1)}, bf16[1,1,40,1024]{3,2,1,0:T(8,128)(2,1)}, u32[]{:S(2)}) copy-start(bf16[1,1,40,1024]{3,2,1,0:T(8,128)(2,1)} %copy.69) | copy-start | bytes 245764
  191.2 9.3 %copy-start.10 = (bf16[1,1,40,1024]{3,2,1,0:T(8,128)(2,1)S(1)}, bf16[1,1,40,1024]{3,2,1,0:T(8,128)(2,1)}, u32[]{:S(2)}) copy-start(bf16[1,1,40,1024]{3,2,1,0:T(8,128)(2,1)} %copy.70) | copy-start | bytes 245764
  305.2 99.5 %all-to-all-start.2 = ((f32[8,40,1280]{2,1,0:T(8,128)}), f32[8,40,1280]{2,1,0:T(8,128)}, u32[]{:S(2)}, u32[]{:S(2)}) async-start(f32[8,40,1280]{2,1,0:T(8,128)} %broadcast_in_dim.26), calls=%async_computation.2 | async-start | bytes 3276800 | tf_op jit(solution)/shard_map/all_to_all | solution.py:16
  400.5 4.2 %copy-start.17 = (f32[4,1280]{1,0:T(4,128)}, f32[4,1280]{1,0:T(4,128)S(1)}, u32[]{:S(2)}) copy-start(f32[4,1280]{1,0:T(4,128)S(1)} %psum.7) | copy-start | bytes 61444
Sparse Core Ops, SparseCore 0:
  9.8 88.0 all-gather.1
  144.3 158.6 reduce-scatter.3
